TPU v7x, 256 devices: a whole 4x4x8 slice. The times are simulated.
256 devices in a mesh: expert: 32 (over z, y), etp: 8 (over x, core).
Axes of the slice: x: 4, y: 4, z: 8, core: 2. Of those that a mesh axis runs over, the one named last changes fastest.
Arguments:
- tokens: bfloat16 [32768, 2560], P(('expert', 'etp')), may hold values from -6 to 6
- grad_out: bfloat16 [32768, 2560], P(('expert', 'etp')), may hold values from -6 to 6
- router_weight: bfloat16 [2560, 32], replicated, may hold values from -0.125 to 0.125
- expert_choice: int32 [32768, 1], P(('expert', 'etp')), may hold values from 0 to 31; in each aligned block of 128 rows (0 to 127, 128 to 255, ...) at most 6 rows name the same one
- gate_pre: bfloat16 [32, 1536, 4096], P('expert', None, 'etp'), may hold values from -6 to 6
- up_pre: bfloat16 [32, 1536, 4096], P('expert', None, 'etp'), may hold values from -6 to 6
- w_gate: bfloat16 [32, 2560, 4096], P('expert', None, 'etp'), may hold values from -0.125 to 0.125
- w_up: bfloat16 [32, 2560, 4096], P('expert', None, 'etp'), may hold values from -0.125 to 0.125
- w_down: bfloat16 [32, 4096, 2560], P('expert', 'etp'), may hold values from -0.09375 to 0.09375
Outputs:
- token_grad: bfloat16 [32768, 2560], P(('expert', 'etp'))
- router_grad: float32 [2560, 32], replicated
Inputs may be any that keep to these rules, and one draw needn't show every extreme that they name: `expert_choice`: within the 128 tokens of one device no expert is chosen more than 6 times, and in every draw some expert is chosen exactly 6 times by the tokens of some device.
All inputs are finite; a program needn't handle non-finite values.
Results may differ from a plain program's by a relative error of at most 0.015.
Values may be sent and summed in bfloat16 or wider, within the bound.
No kernel may reach another device: no remote copies, remote signals or barrier semaphores. Data moves between devices by JAX's collectives and lax.ppermute only.
A program may use at most 128 MiB of HBM per device.

v0:
```python
import jax
import jax.numpy as jnp
from jax import lax
from jax.sharding import PartitionSpec as P


def local(tokens, grad_out, router_weight, expert_choice, gate_pre, up_pre, w_gate, w_up, w_down):
    width = tokens.shape[1]
    experts = router_weight.shape[1]
    n_expert = lax.axis_size("expert")
    n_etp = lax.axis_size("etp")
    capacity = gate_pre.shape[1] // (n_expert * n_etp)
    contract = (((1,), (1,)), ((), ()))
    chosen_ids = expert_choice[:, 0]
    picked = chosen_ids[:, None] == jnp.arange(experts, dtype=jnp.int32)[None, :]
    logits = jnp.dot(tokens, router_weight, preferred_element_type=jnp.float32)
    score = jax.nn.sigmoid(jnp.sum(jnp.where(picked, logits, 0.0), axis=1))
    counts = picked.astype(jnp.int32)
    earlier = jnp.cumsum(counts, axis=0) - counts
    position = jnp.sum(earlier * counts, axis=1)
    target = chosen_ids * capacity + position
    placed = jnp.arange(experts * capacity, dtype=jnp.int32)[:, None] == target[None, :]
    onehot = placed.astype(jnp.bfloat16)
    outgoing = jnp.dot(onehot, grad_out, preferred_element_type=jnp.float32).astype(jnp.bfloat16)
    own = lax.all_to_all(outgoing, "expert", split_axis=0, concat_axis=0, tiled=True)
    arrived = lax.all_gather(own, "etp", axis=0, tiled=True)
    d_hidden = lax.dot_general(arrived, w_down[0], contract, preferred_element_type=jnp.float32)
    gate_f = gate_pre[0].astype(jnp.float32)
    up_f = up_pre[0].astype(jnp.float32)
    sig = jax.nn.sigmoid(gate_f)
    d_gate = (d_hidden * up_f * sig * (1.0 + gate_f * (1.0 - sig))).astype(jnp.bfloat16)
    d_up = (d_hidden * gate_f * sig).astype(jnp.bfloat16)
    terms = (
        lax.dot_general(d_gate, w_gate[0], contract, preferred_element_type=jnp.float32)
        + lax.dot_general(d_up, w_up[0], contract, preferred_element_type=jnp.float32)
    ).astype(jnp.bfloat16)
    summed = lax.psum_scatter(terms, "etp", scatter_dimension=0, tiled=True)
    returned = lax.all_to_all(summed, "expert", split_axis=0, concat_axis=0, tiled=True)
    fetched = lax.dot_general(
        onehot, returned, (((0,), (0,)), ((), ())), preferred_element_type=jnp.float32
    )
    inputs = tokens.astype(jnp.float32)
    d_logit = jnp.sum(inputs * fetched, axis=1) * score * (1.0 - score)
    column = lax.dot_general(
        picked.astype(jnp.bfloat16), router_weight, contract, preferred_element_type=jnp.float32
    )
    token_grad = (score[:, None] * fetched + d_logit[:, None] * column).astype(jnp.bfloat16)
    weighted = jnp.where(picked, d_logit[:, None], 0.0)
    local_terms = lax.dot_general(
        weighted,
        inputs,
        (((0,), (0,)), ((), ())),
        precision=lax.Precision.HIGHEST,
        preferred_element_type=jnp.float32,
    )
    mine = lax.all_to_all(
        local_terms.reshape(n_etp, experts // n_etp, width),
        "etp",
        split_axis=0,
        concat_axis=0,
        tiled=True,
    )
    mine = jnp.sum(mine, axis=0)
    mine = lax.psum(mine, "expert")
    router_grad = lax.all_gather(mine, "etp", axis=0, tiled=True).T
    return (token_grad, router_grad)


def solution(mesh):
    placed = (
        P(("expert", "etp"), None),
        P(("expert", "etp"), None),
        P(),
        P(("expert", "etp"), None),
        P("expert", None, "etp"),
        P("expert", None, "etp"),
        P("expert", None, "etp"),
        P("expert", None, "etp"),
        P("expert", "etp", None),
    )
    return jax.shard_map(
        local,
        mesh=mesh,
        in_specs=placed,
        out_specs=(P(("expert", "etp"), None), P()),
        check_vma=False,
    )
```

profile of v0, /device:TPU:1, one launch (start us, length us, event | category | flops | bytes accessed | tf_op | source)
XLA Modules:
  0.0 423.1 jit_solution(13606596880845416231)
XLA Ops:
  7.2 0.8 fusion.29
  8.0 0.1 copy.15
  8.1 0.2 reduce_window_sum.11
  8.3 0.1 copy.16
  8.4 0.7 select_reduce_fusion
  9.1 0.7 multiply_add_fusion
  9.7 2.5 convolution_convert_fusion
  12.2 2.3 all_to_all.19
  14.4 46.0 %all_to_all.29 = bf16[32,6,2560]{2,1,0:T(8,128)(2,1)} all-to-all(bf16[32,6,2560]{2,1,0:T(8,128)(2,1)} %all_to_all.19), channel_id=1, replica_groups=mesh['expert'=32,'etp'=8] {'expert'}, dimensions={0} | all-to-all | bytes 1966080 | tf_op jit(solution)/shard_map/all_to_all | solution.py:25
  60.4 2.3 all_to_all.21
  62.7 0.0 reduce-scatter.2.cloned.1.call-start
  62.8 47.8 %all-gather.3.cloned.1.call-done = bf16[1536,2560]{1,0:T(8,128)(2,1)} async-done(((bf16[192,2560]{1,0:T(8,128)(2,1)}), bf16[1536,2560]{1,0:T(8,128)(2,1)}) %all-gather.3.cloned.1.call-update) | async-done | bytes 7864336 | tf_op jit(solution)/shard_map/all_gather | solution.py:26
  110.6 7.5 %fusion.14 = f32[1536,512]{1,0:T(8,128)S(1)} fusion(bf16[1536,2560]{1,0:T(8,128)(2,1)} %all-gather.3.cloned.1.call-done, bf16[1,512,2560]{2,1,0:T(8,128)(2,1)} %param.17), kind=kOutput, calls=%fused_computation.21 | convolution fusion | flops 4026531840 | bytes 13631488 | tf_op jit(solution)/shard_map/dot_general | solution.py:27
  118.1 1.7 copy-done.6
  119.8 9.8 %fusion.12 = f32[1536,2560]{1,0:T(8,128)} fusion(bf16[1,2560,512]{2,1,0:T(8,128)(2,1)S(1)} %copy-done, f32[1536,512]{1,0:T(8,128)S(1)} %fusion.14, bf16[1,1536,512]{2,1,0:T(8,128)(2,1)S(1)} %copy-done.4, bf16[1,1536,512]{2,1,0:T(8,128)(2,1)S(1)} %copy-done.5), kind=kOutput, calls=%fused_computation.19 | convolution fusion | flops 4035969024 | bytes 24641536 | tf_op jit(solution)/shard_map/dot_general | solution.py:34
  129.6 15.2 %add_convert_fusion = bf16[1536,2560]{1,0:T(8,128)(2,1)} fusion(f32[1536,2560]{1,0:T(8,128)} %fusion.12, bf16[1,2560,512]{2,1,0:T(8,128)(2,1)} %param.16, f32[1536,512]{1,0:T(8,128)} %copy-done.6, bf16[1,1536,512]{2,1,0:T(8,128)(2,1)} %param.13), kind=kOutput, calls=%fused_computation | convolution fusion | flops 4039901184 | bytes 30932992 | tf_op jit(solution)/shard_map/dot_general | solution.py:35
  144.9 51.8 %reduce-scatter.2.cloned.1.call-done = bf16[192,2560]{1,0:T(8,128)(2,1)} async-done(((bf16[1536,2560]{1,0:T(8,128)(2,1)}), bf16[192,2560]{1,0:T(8,128)(2,1)}) %reduce-scatter.2.cloned.1.call-update) | async-done | bytes 983056 | tf_op jit(solution)/shard_map/reduce_scatter | solution.py:37
  196.8 2.3 all_to_all.22
  199.0 9.7 %all-to-all-start.1 = ((bf16[32,6,2560]{2,1,0:T(8,128)(2,1)}), bf16[32,6,2560]{2,1,0:T(8,128)(2,1)}, u32[]{:S(2)}, u32[]{:S(2)}) async-start(bf16[32,6,2560]{2,1,0:T(8,128)(2,1)} %all_to_all.22), calls=%async_computation.2 | async-start | bytes 2621440 | tf_op jit(solution)/shard_map/all_to_all | solution.py:38
  208.8 0.3 fusion.23
  209.1 30.4 %all-to-all-done.1 = bf16[32,6,2560]{2,1,0:T(8,128)(2,1)} async-done(((bf16[32,6,2560]{2,1,0:T(8,128)(2,1)}), bf16[32,6,2560]{2,1,0:T(8,128)(2,1)}, u32[]{:S(2)}, u32[]{:S(2)}) %all-to-all-start.1) | async-done | bytes 983072 | tf_op jit(solution)/shard_map/all_to_all | solution.py:38
  239.5 2.2 all_to_all.24
  241.7 2.7 multiply_reduce_fusion
  244.4 1.1 fusion.27
  245.5 1.8 reshape.36
  247.3 7.3 %all-to-all-start.2 = ((f32[8,4,2560]{2,1,0:T(4,128)}), f32[8,4,2560]{2,1,0:T(4,128)S(1)}, u32[]{:S(2)}, u32[]{:S(2)}) async-start(f32[8,4,2560]{2,1,0:T(4,128)} %reshape.36), calls=%async_computation.3 | async-start | bytes 655360 | tf_op jit(solution)/shard_map/all_to_all | solution.py:56
  254.6 2.5 fusion.1
  257.1 4.6 %all-to-all-done.2 = f32[8,4,2560]{2,1,0:T(4,128)S(1)} async-done(((f32[8,4,2560]{2,1,0:T(4,128)}), f32[8,4,2560]{2,1,0:T(4,128)S(1)}, u32[]{:S(2)}, u32[]{:S(2)}) %all-to-all-start.2) | async-done | bytes 327712 | tf_op jit(solution)/shard_map/all_to_all | solution.py:56
  261.7 0.1 reduce_sum.39
  261.8 112.4 %psum.7 = f32[4,2560]{1,0:T(4,128)S(1)} all-reduce(f32[4,2560]{1,0:T(4,128)S(1)} %reduce_sum.39), channel_id=1, replica_groups=mesh['expert'=32,'etp'=8] {'expert'}, use_global_device_ids=true, to_apply=%region_6.7 | all-reduce | flops 10240 | bytes 81920 | tf_op jit(solution)/shard_map/psum | solution.py:64
  374.2 41.3 %all-gather = f32[8,4,2560]{2,1,0:T(4,128)S(1)} all-gather(f32[1,4,2560]{2,1,0:T(4,128)S(1)} %bitcast.37), channel_id=1, replica_groups=mesh['expert'=32,'etp'=8] {'etp'}, dimensions={0}, use_global_device_ids=true | all-gather | bytes 368640 | tf_op jit(solution)/shard_map/all_gather | solution.py:65
  415.5 0.8 reshape.40
  (17 shorter events, 0.1 us)
Async XLA Ops:
  7.2 112.6 %copy-start = (bf16[1,2560,512]{2,1,0:T(8,128)(2,1)S(1)}, bf16[1,2560,512]{2,1,0:T(8,128)(2,1)}, u32[]{:S(2)}) copy-start(bf16[1,2560,512]{2,1,0:T(8,128)(2,1)} %param.15) | copy-start | bytes 7864324
  7.2 103.4 %all-gather.3.cloned.1.call-start = ((), (), s32[]{:S(2)}) async-start(), calls=%async_computation.4 | async-start | bytes 8847360 | tf_op jit(solution)/shard_map/all_gather | solution.py:26
  62.7 134.0 %reduce-scatter.2.cloned.1.call-start = ((), (), s32[]{:S(2)}) async-start(), calls=%async_computation.5 | async-start | bytes 8847360 | tf_op jit(solution)/shard_map/reduce_scatter | solution.py:37
  110.6 9.3 %copy-start.4 = (bf16[1,1536,512]{2,1,0:T(8,128)(2,1)S(1)}, bf16[1,1536,512]{2,1,0:T(8,128)(2,1)}, u32[]{:S(2)}) copy-start(bf16[1,1536,512]{2,1,0:T(8,128)(2,1)} %param.14) | copy-start | bytes 4718596
  110.6 9.3 %copy-start.5 = (bf16[1,1536,512]{2,1,0:T(8,128)(2,1)S(1)}, bf16[1,1536,512]{2,1,0:T(8,128)(2,1)}, u32[]{:S(2)}) copy-start(bf16[1,1536,512]{2,1,0:T(8,128)(2,1)} %param.13) | copy-start | bytes 4718596
  118.1 1.7 copy-start.6
  144.9 63.8 %copy-start.1 = (bf16[128,2560]{1,0:T(8,128)(2,1)S(1)}, bf16[128,2560]{1,0:T(8,128)(2,1)}, u32[]{:S(2)}) copy-start(bf16[128,2560]{1,0:T(8,128)(2,1)} %param.9) | copy-start | bytes 1966084
  144.9 63.8 %copy-start.2 = (bf16[2560,32]{0,1:T(8,128)(2,1)S(1)}, bf16[2560,32]{0,1:T(8,128)(2,1)}, u32[]{:S(2)}) copy-start(bf16[2560,32]{0,1:T(8,128)(2,1)} %param.11) | copy-start | bytes 491524
  144.9 63.8 %copy-start.3 = (s32[128,1]{0,1:T(1,128)S(1)}, s32[128,1]{0,1:T(1,128)}, u32[]{:S(2)}) copy-start(s32[128,1]{0,1:T(1,128)} %param.12) | copy-start | bytes 1540
  199.0 40.4 %all-to-all-start.1 = ((bf16[32,6,2560]{2,1,0:T(8,128)(2,1)}), bf16[32,6,2560]{2,1,0:T(8,128)(2,1)}, u32[]{:S(2)}, u32[]{:S(2)}) async-start(bf16[32,6,2560]{2,1,0:T(8,128)(2,1)} %all_to_all.22), calls=%async_computation.2 | async-start | bytes 2621440 | tf_op jit(solution)/shard_map/all_to_all | solution.py:38
  247.3 14.4 %all-to-all-start.2 = ((f32[8,4,2560]{2,1,0:T(4,128)}), f32[8,4,2560]{2,1,0:T(4,128)S(1)}, u32[]{:S(2)}, u32[]{:S(2)}) async-start(f32[8,4,2560]{2,1,0:T(4,128)} %reshape.36), calls=%async_computation.3 | async-start | bytes 655360 | tf_op jit(solution)/shard_map/all_to_all | solution.py:56
Sparse Core Ops, SparseCore 0:
  62.9 47.6 all-gather.2
  145.0 51.6 reduce-scatter.1
where the time goes:
time: 424 us; the launch traced here: 423 us
  blocking collectives  200 us (47%)
  waiting for transfers between devices  135 us (32%)
  matrix products  41.7 us (10%)
  starting transfers between devices  17.1 us (4%)
  between operations  14.1 us (3%)
  local copies, waits for them, and re-layouts  13.6 us (3%)
    psum x1, blocking collectives, local(): mine = lax.psum(mine, 'expert')  112 us
    reduce_scatter x1, waiting for transfers between devices, local(): summed = lax.psum_scatter(terms, 'etp', scatter_dimension=0, tiled=True)  51.8 us
    all_gather x1, waiting for transfers between devices, local(): arrived = lax.all_gather(own, 'etp', axis=0, tiled=True)  47.8 us
    all_to_all x1, blocking collectives, local(): lax.all_to_all(outgoing, 'expert', split_axis=0, concat_axis=0, tiled=True)  46 us
    all_gather x1, blocking collectives, local(): router_grad = lax.all_gather(mine, 'etp', axis=0, tiled=True).T  41.3 us
    all_to_all x1, waiting for transfers between devices, local(): lax.all_to_all(summed, 'expert', split_axis=0, concat_axis=0, tiled=True)  30.4 us
    dot_general x1, matrix products, local(): lax.dot_general(d_up, w_up[0], contract, preferred_element_type=jnp.float32)  15.2 us
    dot_general x1, matrix products, local(): lax.dot_general(d_gate, w_gate[0], contract, preferred_element_type=jnp.f...  9.81 us
  transfers between devices with their start and end apart: 4, of which 4 were waited for; matrix products, arithmetic and copies ran while one was open for 1% of the time, Pallas kernels for 0%

commit v1 on v0

--- a/solution.py
+++ b/solution.py
@@ -61,7 +61,17 @@
         tiled=True,
     )
     mine = jnp.sum(mine, axis=0)
-    mine = lax.psum(mine, "expert")
+
+    def panels_lead(in_array):
+        dev_axis = "expert"
+        world = lax.axis_size(dev_axis)
+        current_value = lambda mat_out: [(nth, nth ^ mat_out) for nth in range(world)]
+        m_next = in_array
+        for u in range(world.bit_length() - 1):
+            m_next = m_next + lax.ppermute(m_next, dev_axis, perm=current_value(1 << u))
+        return m_next
+
+    mine = panels_lead(mine)
     router_grad = lax.all_gather(mine, "etp", axis=0, tiled=True).T
     return (token_grad, router_grad)
 

time: 424 us -> 311 us (0.73)
  blocking collectives: 200 us -> 80.9 us
    psum x1 -> x0, blocking collectives: 112 us -> none  [local(): mine = lax.psum(mine, 'expert')]
    all_gather x1, blocking collectives: 41.3 us -> 20.4 us  [local(): router_grad = lax.all_gather(mine, 'etp', axis=0, tiled=True).T]
    all_to_all x0 -> x1, blocking collectives: none -> 14.6 us  [local(): lax.all_to_all(local_terms.reshape(n_etp, experts // n_etp, width), 'etp'...]
    ppermute x0 -> x5, starting transfers between devices: none -> 10.1 us  [panels_lead(): m_next = m_next + lax.ppermute(m_next, dev_axis, perm=current_value(1 << u))]
    ppermute x0 -> x5, waiting for transfers between devices: none -> 8.71 us  [panels_lead(): m_next = m_next + lax.ppermute(m_next, dev_axis, perm=current_value(1 << u))]
    all_to_all x1 -> x0, starting transfers between devices: 7.3 us -> none  [local(): lax.all_to_all(local_terms.reshape(n_etp, experts // n_etp, width), 'etp'...]
    all_to_all x1 -> x0, waiting for transfers between devices: 4.58 us -> none  [local(): lax.all_to_all(local_terms.reshape(n_etp, experts // n_etp, width), 'etp'...]
  transfers between devices with their start and end apart: 4 -> 8, of which waited for: 4 -> 8; matrix products, arithmetic and copies ran while one was open for 1% -> 1% of each run, Pallas kernels for 0% -> 0%
where the time goes in v1:
time: 311 us
  waiting for transfers between devices  139 us (45%)
  blocking collectives  80.9 us (26%)
  matrix products  41.7 us (13%)
  starting transfers between devices  19.8 us (6%)
  between operations  14.2 us (5%)
  local copies, waits for them, and re-layouts  12.9 us (4%)
    reduce_scatter x1, waiting for transfers between devices, local(): summed = lax.psum_scatter(terms, 'etp', scatter_dimension=0, tiled=True)  51.8 us
    all_gather x1, waiting for transfers between devices, local(): arrived = lax.all_gather(own, 'etp', axis=0, tiled=True)  47.8 us
    all_to_all x1, blocking collectives, local(): lax.all_to_all(outgoing, 'expert', split_axis=0, concat_axis=0, tiled=True)  46 us
    all_to_all x1, waiting for transfers between devices, local(): lax.all_to_all(summed, 'expert', split_axis=0, concat_axis=0, tiled=True)  30.4 us
    all_gather x1, blocking collectives, local(): router_grad = lax.all_gather(mine, 'etp', axis=0, tiled=True).T  20.4 us
    dot_general x1, matrix products, local(): lax.dot_general(d_up, w_up[0], contract, preferred_element_type=jnp.float32)  15.3 us
    all_to_all x1, blocking collectives, local(): lax.all_to_all(local_terms.reshape(n_etp, experts // n_etp, width), 'etp'...  14.6 us
    ppermute x5, starting transfers between devices, panels_lead(): m_next = m_next + lax.ppermute(m_next, dev_axis, perm=current_value(1 << u))  10.1 us
  transfers between devices with their start and end apart: 8, of which 8 were waited for; matrix products, arithmetic and copies ran while one was open for 1% of the time, Pallas kernels for 0%

profile of v1, /device:TPU:1, one launch (start us, length us, event | category | flops | bytes accessed | tf_op | source)
XLA Modules:
  0.0 310.7 jit_solution(4350975677315968192)
XLA Ops:
  7.2 0.8 fusion.29
  9.7 2.5 convolution_convert_fusion
  12.2 2.3 all_to_all.19
  14.5 46.0 %all_to_all.29 = bf16[32,6,2560]{2,1,0:T(8,128)(2,1)} all-to-all(bf16[32,6,2560]{2,1,0:T(8,128)(2,1)} %all_to_all.19), channel_id=1, replica_groups=mesh['expert'=32,'etp'=8] {'expert'}, dimensions={0} | all-to-all | bytes 1966080 | tf_op jit(solution)/shard_map/all_to_all | solution.py:25
  60.4 2.3 all_to_all.21
  62.8 47.8 %all-gather.3.cloned.1.call-done = bf16[1536,2560]{1,0:T(8,128)(2,1)} async-done(((bf16[192,2560]{1,0:T(8,128)(2,1)}), bf16[1536,2560]{1,0:T(8,128)(2,1)}) %all-gather.3.cloned.1.call-update) | async-done | bytes 7864336 | tf_op jit(solution)/shard_map/all_gather | solution.py:26
  110.6 7.5 %fusion.14 = f32[1536,512]{1,0:T(8,128)S(1)} fusion(bf16[1536,2560]{1,0:T(8,128)(2,1)} %all-gather.3.cloned.1.call-done, bf16[1,512,2560]{2,1,0:T(8,128)(2,1)} %param.17), kind=kOutput, calls=%fused_computation.21 | convolution fusion | flops 4026531840 | bytes 13631488 | tf_op jit(solution)/shard_map/dot_general | solution.py:27
  118.1 1.7 copy-done.6
  119.8 9.8 %fusion.12 = f32[1536,2560]{1,0:T(8,128)} fusion(bf16[1,2560,512]{2,1,0:T(8,128)(2,1)S(1)} %copy-done, f32[1536,512]{1,0:T(8,128)S(1)} %fusion.14, bf16[1,1536,512]{2,1,0:T(8,128)(2,1)S(1)} %copy-done.4, bf16[1,1536,512]{2,1,0:T(8,128)(2,1)S(1)} %copy-done.5), kind=kOutput, calls=%fused_computation.19 | convolution fusion | flops 4035969024 | bytes 24641536 | tf_op jit(solution)/shard_map/dot_general | solution.py:34
  129.7 15.3 %add_convert_fusion = bf16[1536,2560]{1,0:T(8,128)(2,1)} fusion(f32[1536,2560]{1,0:T(8,128)} %fusion.12, bf16[1,2560,512]{2,1,0:T(8,128)(2,1)} %param.16, f32[1536,512]{1,0:T(8,128)} %copy-done.6, bf16[1,1536,512]{2,1,0:T(8,128)(2,1)} %param.13), kind=kOutput, calls=%fused_computation | convolution fusion | flops 4039901184 | bytes 30932992 | tf_op jit(solution)/shard_map/dot_general | solution.py:35
  145.0 51.8 %reduce-scatter.2.cloned.1.call-done = bf16[192,2560]{1,0:T(8,128)(2,1)} async-done(((bf16[1536,2560]{1,0:T(8,128)(2,1)}), bf16[192,2560]{1,0:T(8,128)(2,1)}) %reduce-scatter.2.cloned.1.call-update) | async-done | bytes 983056 | tf_op jit(solution)/shard_map/reduce_scatter | solution.py:37
  196.8 2.3 all_to_all.22
  199.0 9.7 %all-to-all-start.1 = ((bf16[32,6,2560]{2,1,0:T(8,128)(2,1)}), bf16[32,6,2560]{2,1,0:T(8,128)(2,1)}, u32[]{:S(2)}, u32[]{:S(2)}) async-start(bf16[32,6,2560]{2,1,0:T(8,128)(2,1)} %all_to_all.22), calls=%async_computation.2 | async-start | bytes 2621440 | tf_op jit(solution)/shard_map/all_to_all | solution.py:38
  209.1 30.4 %all-to-all-done.1 = bf16[32,6,2560]{2,1,0:T(8,128)(2,1)} async-done(((bf16[32,6,2560]{2,1,0:T(8,128)(2,1)}), bf16[32,6,2560]{2,1,0:T(8,128)(2,1)}, u32[]{:S(2)}, u32[]{:S(2)}) %all-to-all-start.1) | async-done | bytes 983072 | tf_op jit(solution)/shard_map/all_to_all | solution.py:38
  239.5 2.3 all_to_all.24
  241.7 2.7 multiply_reduce_fusion
  244.4 1.1 fusion.27
  245.5 1.1 reshape.36
  246.6 14.6 %all_to_all.30 = f32[8,4,2560]{2,1,0:T(4,128)S(1)} all-to-all(f32[8,4,2560]{2,1,0:T(4,128)S(1)} %reshape.36), channel_id=1, replica_groups=mesh['expert'=32,'etp'=8] {'etp'}, dimensions={0} | all-to-all | bytes 655360 | tf_op jit(solution)/shard_map/all_to_all | solution.py:56
  261.2 1.3 collective-permute-start
  262.5 1.9 collective-permute-done
  264.4 2.8 collective-permute-start.1
  267.2 1.7 collective-permute-done.1
  268.8 1.0 collective-permute-start.2
  269.8 2.0 collective-permute-done.2
  271.8 2.4 collective-permute-start.3
  274.2 1.5 collective-permute-done.3
  275.7 2.6 collective-permute-start.4
  278.3 2.5 fusion.1
  280.9 1.7 collective-permute-done.4
  282.6 20.4 %all-gather = f32[8,4,2560]{2,1,0:T(4,128)S(1)} all-gather(f32[1,4,2560]{2,1,0:T(4,128)S(1)} %add_bitcast_fusion), channel_id=1, replica_groups=mesh['expert'=32,'etp'=8] {'etp'}, dimensions={0}, use_global_device_ids=true | all-gather | bytes 368640 | tf_op jit(solution)/shard_map/all_gather | solution.py:75
  303.0 0.8 reshape.40
  (30 shorter events, 2.3 us)
Async XLA Ops:
  7.2 112.7 %copy-start = (bf16[1,2560,512]{2,1,0:T(8,128)(2,1)S(1)}, bf16[1,2560,512]{2,1,0:T(8,128)(2,1)}, u32[]{:S(2)}) copy-start(bf16[1,2560,512]{2,1,0:T(8,128)(2,1)} %param.15) | copy-start | bytes 7864324
  7.2 103.4 %all-gather.3.cloned.1.call-start = ((), (), s32[]{:S(2)}) async-start(), calls=%async_computation.4 | async-start | bytes 8847360 | tf_op jit(solution)/shard_map/all_gather | solution.py:26
  62.7 134.1 %reduce-scatter.2.cloned.1.call-start = ((), (), s32[]{:S(2)}) async-start(), calls=%async_computation.5 | async-start | bytes 8847360 | tf_op jit(solution)/shard_map/reduce_scatter | solution.py:37
  110.6 9.3 %copy-start.4 = (bf16[1,1536,512]{2,1,0:T(8,128)(2,1)S(1)}, bf16[1,1536,512]{2,1,0:T(8,128)(2,1)}, u32[]{:S(2)}) copy-start(bf16[1,1536,512]{2,1,0:T(8,128)(2,1)} %param.14) | copy-start | bytes 4718596
  110.6 9.3 %copy-start.5 = (bf16[1,1536,512]{2,1,0:T(8,128)(2,1)S(1)}, bf16[1,1536,512]{2,1,0:T(8,128)(2,1)}, u32[]{:S(2)}) copy-start(bf16[1,1536,512]{2,1,0:T(8,128)(2,1)} %param.13) | copy-start | bytes 4718596
  118.1 1.7 copy-start.6
  144.9 63.8 %copy-start.1 = (bf16[128,2560]{1,0:T(8,128)(2,1)S(1)}, bf16[128,2560]{1,0:T(8,128)(2,1)}, u32[]{:S(2)}) copy-start(bf16[128,2560]{1,0:T(8,128)(2,1)} %param.9) | copy-start | bytes 1966084
  144.9 63.8 %copy-start.2 = (bf16[2560,32]{0,1:T(8,128)(2,1)S(1)}, bf16[2560,32]{0,1:T(8,128)(2,1)}, u32[]{:S(2)}) copy-start(bf16[2560,32]{0,1:T(8,128)(2,1)} %param.11) | copy-start | bytes 491524
  145.0 63.8 %copy-start.3 = (s32[128,1]{0,1:T(1,128)S(1)}, s32[128,1]{0,1:T(1,128)}, u32[]{:S(2)}) copy-start(s32[128,1]{0,1:T(1,128)} %param.12) | copy-start | bytes 1540
  199.0 40.4 %all-to-all-start.1 = ((bf16[32,6,2560]{2,1,0:T(8,128)(2,1)}), bf16[32,6,2560]{2,1,0:T(8,128)(2,1)}, u32[]{:S(2)}, u32[]{:S(2)}) async-start(bf16[32,6,2560]{2,1,0:T(8,128)(2,1)} %all_to_all.22), calls=%async_computation.2 | async-start | bytes 2621440 | tf_op jit(solution)/shard_map/all_to_all | solution.py:38
  261.2 3.1 %collective-permute-start = (f32[4,2560]{1,0:T(4,128)S(1)}, f32[4,2560]{1,0:T(4,128)S(1)}, u32[]{:S(2)}, u32[]{:S(2)}) collective-permute-start(f32[4,2560]{1,0:T(4,128)S(1)} %reduce_sum.39), channel_id=1, source_target_pairs={{0,8},{8,0},{16,24},{24,16},{32,40},{40,32},{48,56},{56,48},{64,72... | collective-permute-start | bytes 122888 | tf_op jit(solution)/shard_map/ppermute | solution.py:71
  264.4 4.4 %collective-permute-start.1 = (f32[4,2560]{1,0:T(4,128)S(1)}, f32[4,2560]{1,0:T(4,128)S(1)}, u32[]{:S(2)}, u32[]{:S(2)}) collective-permute-start(f32[4,2560]{1,0:T(4,128)S(1)} %add.52), channel_id=1, source_target_pairs={{0,16},{8,24},{16,0},{24,8},{32,48},{40,56},{48,32},{56,40},{64,80... | collective-permute-start | bytes 122888 | tf_op jit(solution)/shard_map/ppermute | solution.py:71
  268.8 2.9 collective-permute-start.2
  271.8 3.9 %collective-permute-start.3 = (f32[4,2560]{1,0:T(4,128)S(1)}, f32[4,2560]{1,0:T(4,128)S(1)}, u32[]{:S(2)}, u32[]{:S(2)}) collective-permute-start(f32[4,2560]{1,0:T(4,128)S(1)} %add.54), channel_id=1, source_target_pairs={{0,64},{8,72},{16,80},{24,88},{32,96},{40,104},{48,112},{56,120},{... | collective-permute-start | bytes 122888 | tf_op jit(solution)/shard_map/ppermute | solution.py:71
  275.7 6.9 %collective-permute-start.4 = (f32[4,2560]{1,0:T(4,128)S(1)}, f32[4,2560]{1,0:T(4,128)S(1)}, u32[]{:S(2)}, u32[]{:S(2)}) collective-permute-start(f32[4,2560]{1,0:T(4,128)S(1)} %add.55), channel_id=1, source_target_pairs={{0,128},{8,136},{16,144},{24,152},{32,160},{40,168},{48,176},{56,1... | collective-permute-start | bytes 122888 | tf_op jit(solution)/shard_map/ppermute | solution.py:71
Sparse Core Ops, SparseCore 0:
  62.9 47.6 all-gather.2
  145.0 51.6 reduce-scatter.1
